TPU v7x, 32 devices: a whole 2x2x4 slice. The times are simulated.
32 devices in a mesh: sub: 32 (over z, y, x, core).
Axes of the slice: x: 2, y: 2, z: 4, core: 2. Of those that a mesh axis runs over, the one named last changes fastest.
Arguments:
- deflation: bfloat16 [32768, 128], P('sub'), may hold values from -0.1875 to 0.1875
- op_tiles: bfloat16 [1536, 128, 128], P('sub'), may hold values from -0.21875 to 0.21875
- tile_cols: int32 [1536], P('sub'), may hold values from 0 to 7
- diag_coef: float32 [32768], P('sub'), may hold values from 1 to 4
- fine_rhs: bfloat16 [32768, 128], P('sub'), may hold values from -6 to 6
- adjacency: int32 [32, 8], P('sub'), may hold values from 0 to 1, as said below
- margin_rows: int32 [32, 8, 512], P('sub'), may hold values from 0 to 1023
Outputs:
- fine_residual: bfloat16 [32768, 128], P('sub')
- coarse_residual: float32 [4096, 128], P('sub')
Inputs may be any that keep to these rules, and one draw needn't show every extreme that they name: Symmetric: adjacency[i, s] equals adjacency[(i + o_s) mod 32, s'] with o_s' = -o_s; every subdomain is coupled to both cycle neighbours (slots of offsets 1 and -1); the degrees of subdomains differ widely.
All inputs are finite; a program needn't handle non-finite values.
Results may differ from a plain program's by a relative error of at most 0.0095.
Values may be sent and summed in bfloat16 or wider, within the bound.
A program may use at most 64 MiB of HBM per device.

v0:
```python
import functools

import jax
import jax.numpy as jnp
from jax import lax
from jax.experimental import pallas as pl
from jax.experimental.pallas import tpu as pltpu
from jax.sharding import PartitionSpec as P

BLK = 128
TPR = 6
OFFSETS = (1, 2, 4, 8, -1, -2, -4, -8)
SEND_ORDER = (2, 6, 1, 5, 0, 4, 3, 7)
TAKE_ORDER = (0, 4, 1, 5, 2, 6, 3, 7)
EARLY = 0
SPREAD_NOW = 4
CHEB_CENTER = 2.5
CHEB_HALF = 1.5
RHO_FIRST = CHEB_HALF / CHEB_CENTER
RHO_SECOND = 1.0 / (2.0 * CHEB_CENTER / CHEB_HALF - RHO_FIRST)

F32 = jnp.float32
BF16 = jnp.bfloat16


def back_of(slot):
    return OFFSETS.index(-OFFSETS[slot])


def mm(left, right):
    return jnp.dot(left, right, preferred_element_type=F32)


def halves(value):
    high = value.astype(BF16)
    return high, (value - high.astype(F32)).astype(BF16)


def columns_of(rows):
    count, width = rows.shape
    padded = jnp.concatenate([rows, jnp.zeros((BLK - count, width), rows.dtype)], axis=0)
    return jnp.transpose(padded)


def kernel(
    n, cols_ref, adj_ref, z_hbm, f_hbm, rows_hbm, diag_hbm, tiles_hbm,
    fine_ref, coarse_ref,
    z_ref, f_ref, rows_ref, diag_ref, tiles_ref, z_send, z_recv, t_send, t_recv, v_send, v_recv, g_ref, t_own, rows_img, turned_img, img_ref, mrg_ref,
    in_sems, send_sems, recv_sems,
):
    slots = len(OFFSETS)
    me = lax.axis_index("sub")
    partner = [lax.rem(me + offset + n, n) for offset in OFFSETS]
    blocks, _, width = z_ref.shape
    local_n = blocks * BLK
    margin = rows_ref.shape[1]

    loads = [
        pltpu.make_async_copy(source, target, in_sems.at[index])
        for index, (source, target) in enumerate(
            (
                (rows_hbm, rows_ref), (z_hbm, z_ref), (f_hbm, f_ref), (diag_hbm, diag_ref),
                (tiles_hbm, tiles_ref),
            )
        )
    ]
    for load in loads:
        load.start()
    barrier = pltpu.get_barrier_semaphore()
    for slot in range(slots):
        pl.semaphore_signal(
            barrier, inc=1, device_id=(partner[slot],), device_id_type=pl.DeviceIdType.MESH
        )

    def outgoing(phase, slot, source, target):
        return pltpu.make_async_remote_copy(
            src_ref=source,
            dst_ref=target.at[back_of(slot)],
            send_sem=send_sems.at[phase, slot],
            recv_sem=recv_sems.at[phase, back_of(slot)],
            device_id=(partner[slot],),
            device_id_type=pl.DeviceIdType.MESH,
        )

    z_copies = [outgoing(0, s, z_send.at[s], z_recv) for s in range(slots)]
    t_copies = [outgoing(1, s, t_send.at[s], t_recv) for s in range(slots)]
    v_copies = [outgoing(2, s, v_send, v_recv) for s in range(slots)]

    for load in loads[:3]:
        load.wait()
    basis = z_ref[...].reshape(local_n, width)
    basis_t = jnp.transpose(basis)
    coarse_rhs = mm(basis_t, f_ref[...])
    first = coarse_rhs / CHEB_CENTER
    first_high, first_low = halves(first)
    rows = rows_ref[...].astype(F32)
    row_cols = columns_of(rows)
    lanes = lax.broadcasted_iota(jnp.int32, (margin, local_n), 1).astype(F32)
    def picks_of(slot):
        return jnp.where(row_cols[:, slot : slot + 1] == lanes, 1.0, 0.0).astype(BF16)

    for place, slot in enumerate(SEND_ORDER):
        z_send[slot, :margin, :] = mm(picks_of(slot), basis).astype(BF16)
        z_send[slot, margin:, :] = first_high
        if place == EARLY:
            pl.semaphore_wait(barrier, slots)
            for earlier in SEND_ORDER[:place]:
                z_copies[earlier].start()
        if place >= EARLY:
            z_copies[slot].start()

    for load in loads[3:]:
        load.wait()
    diag_cols = columns_of(diag_ref[...])

    def image_block(source, block):
        left = jnp.concatenate([tiles_ref[block * TPR + t] for t in range(TPR)], axis=1)
        right = jnp.concatenate(
            [source[cols_ref[block * TPR + t]] for t in range(TPR)], axis=0
        )
        return diag_cols[:, block : block + 1] * source[block].astype(F32) + mm(left, right)

    for block in range(blocks):
        img_ref[block * BLK : (block + 1) * BLK, :] = image_block(z_ref, block).astype(BF16)
    images = img_ref[...]
    for slot in TAKE_ORDER:
        rows_img[slot] = mm(picks_of(slot), images).astype(BF16)
    for slot in range(slots):
        turned_img[slot] = jnp.transpose(rows_img[slot])
    own_block = mm(basis_t, images)
    own_high, own_low = halves(own_block)

    def own_apply(high, low):
        return mm(own_high, high) + (mm(own_low, high) + mm(own_high, low))

    sublanes = lax.broadcasted_iota(jnp.int32, (local_n, margin), 0).astype(F32)

    def spread_rows(slot):
        spread = jnp.where(rows[slot : slot + 1, :] == sublanes, 1.0, 0.0).astype(BF16)
        g_ref[:, slot * width : (slot + 1) * width] = mm(
            spread, z_recv[slot, :margin, :]
        ).astype(BF16)

    for place, slot in enumerate(TAKE_ORDER):
        z_copies[back_of(slot)].wait_recv()
        product = mm(turned_img[slot], z_recv[slot, :margin, :])
        t_own[slot] = product
        t_send[slot] = product.astype(BF16)
        t_copies[slot].start()
        if place < SPREAD_NOW:
            spread_rows(slot)
    image = own_apply(first_high, first_low)
    for slot in TAKE_ORDER[SPREAD_NOW:]:
        spread_rows(slot)

    weights = [adj_ref[0, slot].astype(F32) for slot in range(slots)]
    pair_blocks = [None] * slots
    for slot in TAKE_ORDER:
        t_copies[back_of(slot)].wait_recv()
        pair = (t_own[slot] + jnp.transpose(t_recv[slot].astype(F32))) * (0.5 * weights[slot])
        pair_blocks[slot] = halves(pair)
        remote = z_recv[slot, margin:, :]
        image = image + (mm(pair_blocks[slot][0], remote) + mm(pair_blocks[slot][1], remote))
    resid_one = coarse_rhs - image
    second = (RHO_SECOND * RHO_FIRST) * first + (2.0 * RHO_SECOND / CHEB_HALF) * resid_one
    second_high, second_low = halves(second)
    v_send[...] = second_high
    for slot in SEND_ORDER:
        v_copies[slot].start()

    merged = mm(basis, (first + second).astype(BF16))
    image = own_apply(second_high, second_low)
    coeffs = [None] * slots
    for slot in TAKE_ORDER:
        v_copies[back_of(slot)].wait_recv()
        remote = v_recv[slot]
        image = image + (mm(pair_blocks[slot][0], remote) + mm(pair_blocks[slot][1], remote))
        total = z_recv[slot, margin:, :].astype(F32) + remote.astype(F32)
        coeffs[slot] = (total * weights[slot]).astype(BF16)
    coarse_ref[...] = resid_one - image
    merged = merged + mm(g_ref[...], jnp.concatenate(coeffs, axis=0))
    mrg_ref[...] = merged.astype(BF16).reshape(mrg_ref.shape)
    for block in range(blocks):
        span = slice(block * BLK, (block + 1) * BLK)
        fine_ref[span, :] = (
            f_ref[span, :].astype(F32) - image_block(mrg_ref, block)
        ).astype(BF16)
    for slot in range(slots):
        z_copies[slot].wait_send()
        t_copies[slot].wait_send()
        v_copies[slot].wait_send()


def deliver(fine_in, coarse_in, fine_out, coarse_out):
    fine_out[...] = fine_in[...]
    coarse_out[...] = coarse_in[...]


def per_device(n, deflation, op_tiles, tile_cols, diag_coef, fine_rhs, adjacency, margin_rows):
    local_n, width = deflation.shape
    slots, margin = margin_rows.shape[1:]
    vmem = pl.BlockSpec(memory_space=pltpu.VMEM)
    smem = pl.BlockSpec(memory_space=pltpu.SMEM)
    square = (width, width)
    hbm = pl.BlockSpec(memory_space=pltpu.HBM)
    stacked = (local_n // BLK, BLK, width)
    fine, coarse = pl.pallas_call(
        functools.partial(kernel, n),
        out_shape=(
            jax.ShapeDtypeStruct(fine_rhs.shape, BF16),
            jax.ShapeDtypeStruct((width, fine_rhs.shape[1]), F32),
        ),
        in_specs=[smem, smem, hbm, hbm, hbm, hbm, hbm],
        out_specs=(vmem, vmem),
        scratch_shapes=[
            pltpu.VMEM(stacked, BF16),
            pltpu.VMEM(fine_rhs.shape, BF16),
            pltpu.VMEM((slots, margin), jnp.int32),
            pltpu.VMEM(stacked[:2], F32),
            pltpu.VMEM(op_tiles.shape, BF16),
            pltpu.VMEM((slots, margin + width, width), BF16),
            pltpu.VMEM((slots, margin + width, width), BF16),
            pltpu.VMEM((slots,) + square, BF16),
            pltpu.VMEM((slots,) + square, BF16),
            pltpu.VMEM(square, BF16),
            pltpu.VMEM((slots,) + square, BF16),
            pltpu.VMEM((local_n, slots * width), BF16),
            pltpu.VMEM((slots,) + square, F32),
            pltpu.VMEM((slots, margin, width), BF16),
            pltpu.VMEM((slots, width, margin), BF16),
            pltpu.VMEM((local_n, width), BF16),
            pltpu.VMEM(stacked, BF16),
            pltpu.SemaphoreType.DMA((5,)),
            pltpu.SemaphoreType.DMA((3, slots)),
            pltpu.SemaphoreType.DMA((3, slots)),
        ],
        compiler_params=pltpu.CompilerParams(
            collective_id=0, has_side_effects=True
        ),
    )(
        tile_cols, adjacency, deflation.reshape(stacked), fine_rhs, margin_rows[0],
        diag_coef.reshape(stacked[:2]), op_tiles,
    )
    return pl.pallas_call(
        deliver,
        out_shape=(
            jax.ShapeDtypeStruct(fine.shape, fine.dtype),
            jax.ShapeDtypeStruct(coarse.shape, coarse.dtype),
        ),
        in_specs=[vmem, vmem],
        out_specs=(vmem, vmem),
    )(fine, coarse)


def solution(mesh):
    placed = (
        P("sub", None),
        P("sub", None, None),
        P("sub"),
        P("sub"),
        P("sub", None),
        P("sub", None),
        P("sub", None, None),
    )
    return jax.shard_map(
        functools.partial(per_device, mesh.shape["sub"]),
        mesh=mesh,
        in_specs=placed,
        out_specs=(P("sub", None), P("sub", None)),
        check_vma=False,
    )
```

profile of v0, /device:TPU:0, one launch (start us, length us, event | category | flops | bytes accessed | tf_op | source)
XLA Modules:
  0.0 43.1 jit_solution(5213491645240814527)
XLA Ops:
  0.6 40.8 %shard_map.86 = (bf16[1024,128]{1,0:T(8,128)(2,1)}, f32[128,128]{1,0:T(8,128)}) custom-call(s32[48]{0:T(128)} %cols_ref.1, s32[1,8]{1,0:T(1,128)} %adj_ref.1, bf16[8,128,128]{2,1,0:T(8,128)(2,1)} %bitcast.3, bf16[1024,128]{1,0:T(8,128)(2,1)} %f_hbm.1, s32[8,512]{1,0:T(8,128)} %bitcast.4, f32[8,128]{1,0:T(8,128)} %bitcast.5, bf16[48,128,128]{2,1,0:T(8,128)(2,1)} %tiles_hbm.1), custom_call_target="tpu_custom_call" | custom-call | tf_op jit(solution)/shard_map/pallas_call | solution.py:207
  41.4 1.7 %shard_map.87 = (bf16[1024,128]{1,0:T(8,128)(2,1)}, f32[128,128]{1,0:T(8,128)}) custom-call(bf16[1024,128]{1,0:T(8,128)(2,1)} %get-tuple-element.4.fine_in, f32[128,128]{1,0:T(8,128)} %get-tuple-element.5.coarse_in), custom_call_target="tpu_custom_call" | custom-call | tf_op jit(solution)/shard_map/pallas_call | solution.py:244
where the time goes:
time: 43.4 us; the launch traced here: 43.1 us
  Pallas kernels  42.5 us (98%)
  between operations  0.64 us (1%)
    pallas_call x1, Pallas kernels, per_device(): pl.pallas_call(functools.partial(kernel, n), out_shape=(jax.ShapeDtypeStr...  40.8 us
    pallas_call x1, Pallas kernels, per_device(): pl.pallas_call(deliver, out_shape=(jax.ShapeDtypeStruct(fine.shape, fine....  1.69 us

commit v1 on v0

--- a/solution.py
+++ b/solution.py
@@ -207,8 +207,8 @@
     fine, coarse = pl.pallas_call(
         functools.partial(kernel, n),
         out_shape=(
-            jax.ShapeDtypeStruct(fine_rhs.shape, BF16),
-            jax.ShapeDtypeStruct((width, fine_rhs.shape[1]), F32),
+            pltpu.VMEM(fine_rhs.shape, BF16),
+            pltpu.VMEM((width, fine_rhs.shape[1]), F32),
         ),
         in_specs=[smem, smem, hbm, hbm, hbm, hbm, hbm],
         out_specs=(vmem, vmem),
@@ -235,11 +235,11 @@
             pltpu.SemaphoreType.DMA((3, slots)),
         ],
         compiler_params=pltpu.CompilerParams(
-            collective_id=0, has_side_effects=True
+            collective_id=0, has_side_effects=True, vmem_limit_bytes=41943040
         ),
     )(
-        tile_cols, adjacency, deflation.reshape(stacked), fine_rhs, margin_rows[0],
-        diag_coef.reshape(stacked[:2]), op_tiles,
+        *(pltpu.with_memory_space_constraint(x, pltpu.HBM) for x in (tile_cols, adjacency, deflation.reshape(stacked), fine_rhs, margin_rows[0],
+        diag_coef.reshape(stacked[:2]), op_tiles)),
     )
     return pl.pallas_call(
         deliver,
@@ -249,6 +249,7 @@
         ),
         in_specs=[vmem, vmem],
         out_specs=(vmem, vmem),
+        compiler_params=pltpu.CompilerParams(vmem_limit_bytes=4 * 2**20),
     )(fine, coarse)
 
 

time: 43.4 us -> 41.7 us (0.961)
  Pallas kernels: 42.5 us -> 40.8 us
    pallas_call x1, Pallas kernels: 1.69 us -> 0.74 us  [per_device(): pl.pallas_call(deliver, out_shape=(jax.ShapeDtypeStruct(fine.shape, fine....]
    pallas_call x1, Pallas kernels: 40.8 us -> 40 us  [per_device(): pl.pallas_call(functools.partial(kernel, n), out_shape=(pltpu.VMEM(fine_r...]
where the time goes in v1:
time: 41.7 us; the launch traced here: 41.4 us
  Pallas kernels  40.8 us (98%)
  between operations  0.64 us (2%)
    pallas_call x1, Pallas kernels, per_device(): pl.pallas_call(functools.partial(kernel, n), out_shape=(pltpu.VMEM(fine_r...  40 us

profile of v1, /device:TPU:0, one launch (start us, length us, event | category | flops | bytes accessed | tf_op | source)
XLA Modules:
  0.0 41.4 jit_solution(15599090593355691761)
XLA Ops:
  0.6 40.0 %shard_map.86 = (bf16[1024,128]{1,0:T(8,128)(2,1)S(1)}, f32[128,128]{1,0:T(8,128)S(1)}) custom-call(s32[48]{0:T(128)} %cols_ref.1, s32[1,8]{1,0:T(1,128)} %adj_ref.1, bf16[8,128,128]{2,1,0:T(8,128)(2,1)} %bitcast.3, bf16[1024,128]{1,0:T(8,128)(2,1)} %f_hbm.1, s32[8,512]{1,0:T(8,128)} %bitcast.4, f32[8,128]{1,0:T(8,128)} %bitcast.5, ...), custom_call_target="tpu_custom_call" | custom-call | tf_op jit(solution)/shard_map/pallas_call | solution.py:207
  40.7 0.7 %shard_map.87 = (bf16[1024,128]{1,0:T(8,128)(2,1)}, f32[128,128]{1,0:T(8,128)}) custom-call(bf16[1024,128]{1,0:T(8,128)(2,1)S(1)} %get-tuple-element.4.fine_in, f32[128,128]{1,0:T(8,128)S(1)} %get-tuple-element.5.coarse_in), custom_call_target="tpu_custom_call" | custom-call | tf_op jit(solution)/shard_map/pallas_call | solution.py:244

commit v2 on v1

v2 whole, which is shorter than its diff:
```python
import functools

import jax
import jax.numpy as jnp
from jax import lax
from jax.experimental import pallas as pl
from jax.experimental.pallas import tpu as pltpu
from jax.sharding import PartitionSpec as P

BLK = 128
TPR = 6
OFFSETS = (1, 2, 4, 8, -1, -2, -4, -8)
SEND_ORDER = (2, 6, 1, 5, 0, 4, 3, 7)
TAKE_ORDER = (0, 4, 1, 5, 2, 6, 3, 7)
SPREAD_NOW = 4
GROUP = 2
CHEB_CENTER = 2.5
CHEB_HALF = 1.5
RHO_FIRST = CHEB_HALF / CHEB_CENTER
RHO_SECOND = 1.0 / (2.0 * CHEB_CENTER / CHEB_HALF - RHO_FIRST)

F32 = jnp.float32
BF16 = jnp.bfloat16


def back_of(slot):
    return OFFSETS.index(-OFFSETS[slot])


def mm(left, right):
    return jnp.dot(left, right, preferred_element_type=F32)


def halves(value):
    high = value.astype(BF16)
    return high, (value - high.astype(F32)).astype(BF16)


def columns_of(rows):
    count, width = rows.shape
    padded = jnp.concatenate([rows, jnp.zeros((BLK - count, width), rows.dtype)], axis=0)
    return jnp.transpose(padded)


def kernel(
    n, cols_ref, adj_ref, z_hbm, f_hbm, rows_hbm, diag_hbm, tiles_hbm,
    fine_ref, coarse_ref,
    z_ref, f_ref, rows_ref, diag_ref, tiles_ref, z_send, z_recv, f_send, f_recv, t_send, t_recv, v_send, v_recv,
    g_ref, h_ref, e_ref, t_own, rows_img, turned_img, img_ref, acc_ref,
    in_sems, send_sems, recv_sems,
):
    slots = len(OFFSETS)
    me = lax.axis_index("sub")
    partner = [lax.rem(me + offset + n, n) for offset in OFFSETS]
    blocks, _, width = z_ref.shape
    local_n = blocks * BLK
    margin = rows_ref.shape[1]

    loads = [
        pltpu.make_async_copy(source, target, in_sems.at[index])
        for index, (source, target) in enumerate(
            (
                (rows_hbm, rows_ref), (z_hbm, z_ref), (f_hbm, f_ref), (diag_hbm, diag_ref),
                (tiles_hbm, tiles_ref),
            )
        )
    ]
    for load in loads[:2]:
        load.start()
    barrier = pltpu.get_barrier_semaphore()
    for slot in range(slots):
        pl.semaphore_signal(
            barrier, inc=1, device_id=(partner[slot],), device_id_type=pl.DeviceIdType.MESH
        )
    for load in loads[2:]:
        load.start()

    def outgoing(phase, slot, source, target):
        return pltpu.make_async_remote_copy(
            src_ref=source,
            dst_ref=target.at[back_of(slot)],
            send_sem=send_sems.at[phase, slot],
            recv_sem=recv_sems.at[phase, back_of(slot)],
            device_id=(partner[slot],),
            device_id_type=pl.DeviceIdType.MESH,
        )

    z_copies = [outgoing(0, s, z_send.at[s], z_recv) for s in range(slots)]
    f_copies = [outgoing(1, s, f_send, f_recv) for s in range(slots)]
    t_copies = [outgoing(2, s, t_send.at[s], t_recv) for s in range(slots)]
    v_copies = [outgoing(3, s, v_send, v_recv) for s in range(slots)]

    for load in loads[:2]:
        load.wait()
    basis = z_ref[...].reshape(local_n, width)
    rows = rows_ref[...].astype(F32)
    row_cols = columns_of(rows)
    lanes = lax.broadcasted_iota(jnp.int32, (margin, local_n), 1).astype(F32)

    def picks_of(slot):
        return jnp.where(row_cols[:, slot : slot + 1] == lanes, 1.0, 0.0).astype(BF16)

    for place, slot in enumerate(SEND_ORDER):
        z_send[slot] = mm(picks_of(slot), basis).astype(BF16)
        if place == 0:
            pl.semaphore_wait(barrier, slots)
        z_copies[slot].start()

    loads[2].wait()
    basis_t = jnp.transpose(basis)
    coarse_rhs = mm(basis_t, f_ref[...])
    first = coarse_rhs / CHEB_CENTER
    first_high, first_low = halves(first)
    f_send[...] = first_high
    for slot in SEND_ORDER:
        f_copies[slot].start()

    for load in loads[3:]:
        load.wait()
    diag_cols = columns_of(diag_ref[...])

    def apply_block(source, block, span):
        left = jnp.concatenate([tiles_ref[block * TPR + t] for t in range(TPR)], axis=1)
        right = jnp.concatenate(
            [source[cols_ref[block * TPR + t], :, span] for t in range(TPR)], axis=0
        )
        own = source[block, :, span].astype(F32)
        return (diag_cols[:, block : block + 1] * own + mm(left, right)).astype(BF16)

    for block in range(blocks):
        img_ref[block * BLK : (block + 1) * BLK, :] = apply_block(z_ref, block, slice(0, width))
    images = img_ref[...]
    for slot in TAKE_ORDER:
        rows_img[slot] = mm(picks_of(slot), images).astype(BF16)
    for slot in TAKE_ORDER:
        turned_img[slot] = jnp.transpose(rows_img[slot])
    own_block = mm(basis_t, images)
    own_high, own_low = halves(own_block)

    def own_apply(high, low):
        return mm(own_high, high) + (mm(own_low, high) + mm(own_high, low))

    sublanes = lax.broadcasted_iota(jnp.int32, (local_n, margin), 0).astype(F32)

    def spread_rows(place):
        slot = TAKE_ORDER[place]
        spread = jnp.where(rows[slot : slot + 1, :] == sublanes, 1.0, 0.0).astype(BF16)
        g_ref[:, :, place * width : (place + 1) * width] = (
            mm(spread, z_recv[slot]).astype(BF16).reshape(blocks, BLK, width)
        )

    def spread_image(group):
        span = slice(group * GROUP * width, (group + 1) * GROUP * width)
        for block in range(blocks):
            h_ref[block * BLK : (block + 1) * BLK, span] = apply_block(g_ref, block, span)

    for place, slot in enumerate(TAKE_ORDER):
        z_copies[back_of(slot)].wait_recv()
        product = mm(turned_img[slot], z_recv[slot])
        t_own[slot] = product
        t_send[slot] = product.astype(BF16)
        t_copies[slot].start()
        if place < SPREAD_NOW:
            spread_rows(place)
            if place % GROUP == GROUP - 1:
                spread_image(place // GROUP)
    image = own_apply(first_high, first_low)
    weights = [adj_ref[0, slot].astype(F32) for slot in range(slots)]
    for slot in TAKE_ORDER:
        f_copies[back_of(slot)].wait_recv()
        high, low = halves(t_own[slot] * (0.5 * weights[slot]))
        image = image + (mm(high, f_recv[slot]) + mm(low, f_recv[slot]))
    for slot in TAKE_ORDER:
        t_copies[back_of(slot)].wait_recv()
        image = image + mm(jnp.transpose(t_recv[slot]), f_recv[slot]) * (0.5 * weights[slot])
    resid_one = coarse_rhs - image
    second = (RHO_SECOND * RHO_FIRST) * first + (2.0 * RHO_SECOND / CHEB_HALF) * resid_one
    second_high, second_low = halves(second)
    v_send[...] = second_high
    for slot in SEND_ORDER:
        v_copies[slot].start()

    acc_ref[...] = f_ref[...].astype(F32) - mm(images, (first + second).astype(BF16))
    for slot in TAKE_ORDER:
        pair = (t_own[slot] + jnp.transpose(t_recv[slot]).astype(F32)) * (0.5 * weights[slot])
        high, low = halves(pair)
        e_ref[slot] = jnp.concatenate([high, low], axis=1)
    for place in range(SPREAD_NOW, slots):
        spread_rows(place)
        if place % GROUP == GROUP - 1:
            spread_image(place // GROUP)
    image = own_apply(second_high, second_low)
    for group in range(slots // GROUP):
        coeffs = []
        for slot in TAKE_ORDER[group * GROUP : (group + 1) * GROUP]:
            v_copies[back_of(slot)].wait_recv()
            remote = v_recv[slot]
            image = image + mm(e_ref[slot], jnp.concatenate([remote, remote], axis=0))
            total = f_recv[slot].astype(F32) + remote.astype(F32)
            coeffs.append((total * weights[slot]).astype(BF16))
        span = slice(group * GROUP * width, (group + 1) * GROUP * width)
        rest = acc_ref[...] - mm(h_ref[:, span], jnp.concatenate(coeffs, axis=0))
        if group < slots // GROUP - 1:
            acc_ref[...] = rest
        else:
            fine_ref[...] = rest.astype(BF16)
    coarse_ref[...] = resid_one - image
    for slot in range(slots):
        z_copies[slot].wait_send()
        f_copies[slot].wait_send()
        t_copies[slot].wait_send()
        v_copies[slot].wait_send()


def deliver(fine_in, coarse_in, fine_out, coarse_out):
    fine_out[...] = fine_in[...]
    coarse_out[...] = coarse_in[...]


def per_device(n, deflation, op_tiles, tile_cols, diag_coef, fine_rhs, adjacency, margin_rows):
    local_n, width = deflation.shape
    slots, margin = margin_rows.shape[1:]
    vmem = pl.BlockSpec(memory_space=pltpu.VMEM)
    smem = pl.BlockSpec(memory_space=pltpu.SMEM)
    square = (width, width)
    hbm = pl.BlockSpec(memory_space=pltpu.HBM)
    stacked = (local_n // BLK, BLK, width)
    fine, coarse = pl.pallas_call(
        functools.partial(kernel, n),
        out_shape=(
            pltpu.VMEM(fine_rhs.shape, BF16),
            pltpu.VMEM((width, fine_rhs.shape[1]), F32),
        ),
        in_specs=[smem, smem, hbm, hbm, hbm, hbm, hbm],
        out_specs=(vmem, vmem),
        scratch_shapes=[
            pltpu.VMEM(stacked, BF16),
            pltpu.VMEM(fine_rhs.shape, BF16),
            pltpu.VMEM((slots, margin), jnp.int32),
            pltpu.VMEM(stacked[:2], F32),
            pltpu.VMEM(op_tiles.shape, BF16),
            pltpu.VMEM((slots, margin, width), BF16),
            pltpu.VMEM((slots, margin, width), BF16),
            pltpu.VMEM(square, BF16),
            pltpu.VMEM((slots,) + square, BF16),
            pltpu.VMEM((slots,) + square, BF16),
            pltpu.VMEM((slots,) + square, BF16),
            pltpu.VMEM(square, BF16),
            pltpu.VMEM((slots,) + square, BF16),
            pltpu.VMEM(stacked[:2] + (slots * width,), BF16),
            pltpu.VMEM((local_n, slots * width), BF16),
            pltpu.VMEM((slots, width, 2 * width), BF16),
            pltpu.VMEM((slots,) + square, F32),
            pltpu.VMEM((slots, margin, width), BF16),
            pltpu.VMEM((slots, width, margin), BF16),
            pltpu.VMEM((local_n, width), BF16),
            pltpu.VMEM((local_n, width), F32),
            pltpu.SemaphoreType.DMA((5,)),
            pltpu.SemaphoreType.DMA((4, slots)),
            pltpu.SemaphoreType.DMA((4, slots)),
        ],
        compiler_params=pltpu.CompilerParams(
            collective_id=0, has_side_effects=True, vmem_limit_bytes=41943040
        ),
    )(
        *(
            pltpu.with_memory_space_constraint(operand, pltpu.HBM)
            for operand in (
                tile_cols, adjacency, deflation.reshape(stacked), fine_rhs, margin_rows[0],
                diag_coef.reshape(stacked[:2]), op_tiles,
            )
        ),
    )
    return pl.pallas_call(
        deliver,
        out_shape=(
            jax.ShapeDtypeStruct(fine.shape, fine.dtype),
            jax.ShapeDtypeStruct(coarse.shape, coarse.dtype),
        ),
        in_specs=[vmem, vmem],
        out_specs=(vmem, vmem),
        compiler_params=pltpu.CompilerParams(vmem_limit_bytes=4 * 2**20),
    )(fine, coarse)


def solution(mesh):
    placed = (
        P("sub", None),
        P("sub", None, None),
        P("sub"),
        P("sub"),
        P("sub", None),
        P("sub", None),
        P("sub", None, None),
    )
    return jax.shard_map(
        functools.partial(per_device, mesh.shape["sub"]),
        mesh=mesh,
        in_specs=placed,
        out_specs=(P("sub", None), P("sub", None)),
        check_vma=False,
    )
```

time: 41.7 us -> 39.9 us (0.957)
  Pallas kernels: 40.8 us -> 38.9 us
    pallas_call x1, Pallas kernels: 40 us -> 38.2 us  [per_device(): pl.pallas_call(functools.partial(kernel, n), out_shape=(pltpu.VMEM(fine_r...]
where the time goes in v2:
time: 39.9 us; the launch traced here: 39.6 us
  Pallas kernels  38.9 us (97%)
  between operations  0.64 us (2%)
    pallas_call x1, Pallas kernels, per_device(): pl.pallas_call(functools.partial(kernel, n), out_shape=(pltpu.VMEM(fine_r...  38.2 us

profile of v2, /device:TPU:0, one launch (start us, length us, event | category | flops | bytes accessed | tf_op | source)
XLA Modules:
  0.0 39.6 jit_solution(17880875224617794824)
XLA Ops:
  0.6 38.2 %shard_map.86 = (bf16[1024,128]{1,0:T(8,128)(2,1)S(1)}, f32[128,128]{1,0:T(8,128)S(1)}) custom-call(s32[48]{0:T(128)} %cols_ref.1, s32[1,8]{1,0:T(1,128)} %adj_ref.1, bf16[8,128,128]{2,1,0:T(8,128)(2,1)} %bitcast.3, bf16[1024,128]{1,0:T(8,128)(2,1)} %f_hbm.1, s32[8,512]{1,0:T(8,128)} %bitcast.4, f32[8,128]{1,0:T(8,128)} %bitcast.5, ...), custom_call_target="tpu_custom_call" | custom-call | tf_op jit(solution)/shard_map/pallas_call | solution.py:228
  38.9 0.7 %shard_map.87 = (bf16[1024,128]{1,0:T(8,128)(2,1)}, f32[128,128]{1,0:T(8,128)}) custom-call(bf16[1024,128]{1,0:T(8,128)(2,1)S(1)} %get-tuple-element.4.fine_in, f32[128,128]{1,0:T(8,128)S(1)} %get-tuple-element.5.coarse_in), custom_call_target="tpu_custom_call" | custom-call | tf_op jit(solution)/shard_map/pallas_call | solution.py:274

commit v3 on v2

--- a/solution.py
+++ b/solution.py
@@ -10,9 +10,16 @@
 BLK = 128
 TPR = 6
 OFFSETS = (1, 2, 4, 8, -1, -2, -4, -8)
-SEND_ORDER = (2, 6, 1, 5, 0, 4, 3, 7)
-TAKE_ORDER = (0, 4, 1, 5, 2, 6, 3, 7)
-SPREAD_NOW = 4
+SEND_ORDER = (1, 5, 2, 6, 0, 4, 3, 7)
+TAKE_ORDER = (4, 0, 5, 1, 6, 2, 7, 3)
+LAST_ORDER = (0, 1, 2, 3, 7, 6, 5, 4)
+FLY_ORDER = (0, 1, 2, 3, 4, 5, 6, 7)
+FIRST_ORDER = (0, 1, 2, 3, 4, 5, 6, 7)
+MEET_ORDER = (0, 4, 1, 5, 2, 6, 3, 7)
+EARLY = 1
+TAKE_WORK = ((4,), (0,), (5, 11), (1, 8), (), (), (), ())
+MID_WORK = ()
+LATE_WORK = (6, 2, 7, 3, 9, 10)
 GROUP = 2
 CHEB_CENTER = 2.5
 CHEB_HALF = 1.5
@@ -43,9 +50,9 @@
 
 
 def kernel(
-    n, cols_ref, adj_ref, z_hbm, f_hbm, rows_hbm, diag_hbm, tiles_hbm,
+    n, cols_hbm, adj_hbm, z_hbm, f_hbm, rows_hbm, diag_hbm, tiles_hbm,
     fine_ref, coarse_ref,
-    z_ref, f_ref, rows_ref, diag_ref, tiles_ref, z_send, z_recv, f_send, f_recv, t_send, t_recv, v_send, v_recv,
+    cols_ref, adj_ref, z_ref, f_ref, rows_ref, diag_ref, tiles_ref, z_send, z_recv, f_send, f_recv, t_send, t_recv, v_send, v_recv,
     g_ref, h_ref, e_ref, t_own, rows_img, turned_img, img_ref, acc_ref,
     in_sems, send_sems, recv_sems,
 ):
@@ -61,7 +68,7 @@
         for index, (source, target) in enumerate(
             (
                 (rows_hbm, rows_ref), (z_hbm, z_ref), (f_hbm, f_ref), (diag_hbm, diag_ref),
-                (tiles_hbm, tiles_ref),
+                (tiles_hbm, tiles_ref), (cols_hbm, cols_ref), (adj_hbm, adj_ref),
             )
         )
     ]
@@ -95,16 +102,29 @@
     basis = z_ref[...].reshape(local_n, width)
     rows = rows_ref[...].astype(F32)
     row_cols = columns_of(rows)
-    lanes = lax.broadcasted_iota(jnp.int32, (margin, local_n), 1).astype(F32)
-
-    def picks_of(slot):
-        return jnp.where(row_cols[:, slot : slot + 1] == lanes, 1.0, 0.0).astype(BF16)
-
+    half = local_n // 2
+    folded = row_cols - jnp.where(row_cols >= half, float(half), 0.0)
+    lanes = lax.broadcasted_iota(jnp.int32, (margin, half), 1).astype(F32)
+
+    def folded_in_two(value):
+        return jnp.concatenate([value[:half], value[half:]], axis=1)
+
+    def pick_rows(slot, wide):
+        picks = jnp.where(folded[:, slot : slot + 1] == lanes, 1.0, 0.0).astype(BF16)
+        both = mm(picks, wide)
+        return jnp.where(
+            row_cols[:, slot : slot + 1] < half, both[:, :width], both[:, width:]
+        ).astype(BF16)
+
+    basis_wide = folded_in_two(basis)
     for place, slot in enumerate(SEND_ORDER):
-        z_send[slot] = mm(picks_of(slot), basis).astype(BF16)
-        if place == 0:
+        z_send[slot] = pick_rows(slot, basis_wide)
+        if place == EARLY:
             pl.semaphore_wait(barrier, slots)
-        z_copies[slot].start()
+            for earlier in SEND_ORDER[:place]:
+                z_copies[earlier].start()
+        if place >= EARLY:
+            z_copies[slot].start()
 
     loads[2].wait()
     basis_t = jnp.transpose(basis)
@@ -112,7 +132,7 @@
     first = coarse_rhs / CHEB_CENTER
     first_high, first_low = halves(first)
     f_send[...] = first_high
-    for slot in SEND_ORDER:
+    for slot in FIRST_ORDER:
         f_copies[slot].start()
 
     for load in loads[3:]:
@@ -130,8 +150,9 @@
     for block in range(blocks):
         img_ref[block * BLK : (block + 1) * BLK, :] = apply_block(z_ref, block, slice(0, width))
     images = img_ref[...]
+    images_wide = folded_in_two(images)
     for slot in TAKE_ORDER:
-        rows_img[slot] = mm(picks_of(slot), images).astype(BF16)
+        rows_img[slot] = pick_rows(slot, images_wide)
     for slot in TAKE_ORDER:
         turned_img[slot] = jnp.transpose(rows_img[slot])
     own_block = mm(basis_t, images)
@@ -140,19 +161,34 @@
     def own_apply(high, low):
         return mm(own_high, high) + (mm(own_low, high) + mm(own_high, low))
 
-    sublanes = lax.broadcasted_iota(jnp.int32, (local_n, margin), 0).astype(F32)
-
-    def spread_rows(place):
-        slot = TAKE_ORDER[place]
-        spread = jnp.where(rows[slot : slot + 1, :] == sublanes, 1.0, 0.0).astype(BF16)
-        g_ref[:, :, place * width : (place + 1) * width] = (
-            mm(spread, z_recv[slot]).astype(BF16).reshape(blocks, BLK, width)
-        )
+    sublanes = lax.broadcasted_iota(jnp.int32, (half, margin), 0).astype(F32)
+    folded_rows = rows - jnp.where(rows >= half, float(half), 0.0)
+
+    def spread_rows(slot):
+        place = LAST_ORDER.index(slot)
+        span = slice(place * width, (place + 1) * width)
+        spread = jnp.where(folded_rows[slot : slot + 1, :] == sublanes, 1.0, 0.0).astype(BF16)
+        arrived = z_recv[slot].astype(F32)
+        lower = row_cols[:, slot : slot + 1] < half
+        wide = jnp.concatenate(
+            [jnp.where(lower, arrived, 0.0), jnp.where(lower, 0.0, arrived)], axis=1
+        ).astype(BF16)
+        both = mm(spread, wide).astype(BF16)
+        shape = (blocks // 2, BLK, width)
+        g_ref[: blocks // 2, :, span] = both[:, :width].reshape(shape)
+        g_ref[blocks // 2 :, :, span] = both[:, width:].reshape(shape)
 
     def spread_image(group):
         span = slice(group * GROUP * width, (group + 1) * GROUP * width)
         for block in range(blocks):
             h_ref[block * BLK : (block + 1) * BLK, span] = apply_block(g_ref, block, span)
+
+    def work(items):
+        for item in items:
+            if item < slots:
+                spread_rows(item)
+            else:
+                spread_image(item - slots)
 
     for place, slot in enumerate(TAKE_ORDER):
         z_copies[back_of(slot)].wait_recv()
@@ -160,42 +196,37 @@
         t_own[slot] = product
         t_send[slot] = product.astype(BF16)
         t_copies[slot].start()
-        if place < SPREAD_NOW:
-            spread_rows(place)
-            if place % GROUP == GROUP - 1:
-                spread_image(place // GROUP)
+        work(TAKE_WORK[place])
     image = own_apply(first_high, first_low)
     weights = [adj_ref[0, slot].astype(F32) for slot in range(slots)]
     for slot in TAKE_ORDER:
+        high, low = halves(t_own[slot] * (0.5 * weights[slot]))
+        e_ref[slot, :, :width] = high
+        e_ref[slot, :, width : 2 * width] = low
         f_copies[back_of(slot)].wait_recv()
-        high, low = halves(t_own[slot] * (0.5 * weights[slot]))
         image = image + (mm(high, f_recv[slot]) + mm(low, f_recv[slot]))
-    for slot in TAKE_ORDER:
+    work(MID_WORK)
+    for slot in MEET_ORDER:
         t_copies[back_of(slot)].wait_recv()
-        image = image + mm(jnp.transpose(t_recv[slot]), f_recv[slot]) * (0.5 * weights[slot])
+        turned = (jnp.transpose(t_recv[slot]).astype(F32) * (0.5 * weights[slot])).astype(BF16)
+        e_ref[slot, :, 2 * width :] = turned
+        image = image + mm(turned, f_recv[slot])
     resid_one = coarse_rhs - image
     second = (RHO_SECOND * RHO_FIRST) * first + (2.0 * RHO_SECOND / CHEB_HALF) * resid_one
     second_high, second_low = halves(second)
     v_send[...] = second_high
-    for slot in SEND_ORDER:
+    for slot in FLY_ORDER:
         v_copies[slot].start()
 
     acc_ref[...] = f_ref[...].astype(F32) - mm(images, (first + second).astype(BF16))
-    for slot in TAKE_ORDER:
-        pair = (t_own[slot] + jnp.transpose(t_recv[slot]).astype(F32)) * (0.5 * weights[slot])
-        high, low = halves(pair)
-        e_ref[slot] = jnp.concatenate([high, low], axis=1)
-    for place in range(SPREAD_NOW, slots):
-        spread_rows(place)
-        if place % GROUP == GROUP - 1:
-            spread_image(place // GROUP)
+    work(LATE_WORK)
     image = own_apply(second_high, second_low)
     for group in range(slots // GROUP):
         coeffs = []
-        for slot in TAKE_ORDER[group * GROUP : (group + 1) * GROUP]:
+        for slot in LAST_ORDER[group * GROUP : (group + 1) * GROUP]:
             v_copies[back_of(slot)].wait_recv()
             remote = v_recv[slot]
-            image = image + mm(e_ref[slot], jnp.concatenate([remote, remote], axis=0))
+            image = image + mm(e_ref[slot], jnp.concatenate([remote] * 3, axis=0))
             total = f_recv[slot].astype(F32) + remote.astype(F32)
             coeffs.append((total * weights[slot]).astype(BF16))
         span = slice(group * GROUP * width, (group + 1) * GROUP * width)
@@ -221,7 +252,6 @@
     local_n, width = deflation.shape
     slots, margin = margin_rows.shape[1:]
     vmem = pl.BlockSpec(memory_space=pltpu.VMEM)
-    smem = pl.BlockSpec(memory_space=pltpu.SMEM)
     square = (width, width)
     hbm = pl.BlockSpec(memory_space=pltpu.HBM)
     stacked = (local_n // BLK, BLK, width)
@@ -231,9 +261,11 @@
             pltpu.VMEM(fine_rhs.shape, BF16),
             pltpu.VMEM((width, fine_rhs.shape[1]), F32),
         ),
-        in_specs=[smem, smem, hbm, hbm, hbm, hbm, hbm],
+        in_specs=[hbm, hbm, hbm, hbm, hbm, hbm, hbm],
         out_specs=(vmem, vmem),
         scratch_shapes=[
+            pltpu.SMEM(tile_cols.shape, jnp.int32),
+            pltpu.SMEM(adjacency.shape, jnp.int32),
             pltpu.VMEM(stacked, BF16),
             pltpu.VMEM(fine_rhs.shape, BF16),
             pltpu.VMEM((slots, margin), jnp.int32),
@@ -249,13 +281,13 @@
             pltpu.VMEM((slots,) + square, BF16),
             pltpu.VMEM(stacked[:2] + (slots * width,), BF16),
             pltpu.VMEM((local_n, slots * width), BF16),
-            pltpu.VMEM((slots, width, 2 * width), BF16),
+            pltpu.VMEM((slots, width, 3 * width), BF16),
             pltpu.VMEM((slots,) + square, F32),
             pltpu.VMEM((slots, margin, width), BF16),
             pltpu.VMEM((slots, width, margin), BF16),
             pltpu.VMEM((local_n, width), BF16),
             pltpu.VMEM((local_n, width), F32),
-            pltpu.SemaphoreType.DMA((5,)),
+            pltpu.SemaphoreType.DMA((7,)),
             pltpu.SemaphoreType.DMA((4, slots)),
             pltpu.SemaphoreType.DMA((4, slots)),
         ],

time: 39.9 us -> 37 us (0.927)
  Pallas kernels: 38.9 us -> 36.2 us
    pallas_call x1, Pallas kernels: 38.2 us -> 35.4 us  [per_device(): pl.pallas_call(functools.partial(kernel, n), out_shape=(pltpu.VMEM(fine_r...]
where the time goes in v3:
time: 37 us; the launch traced here: 36.8 us
  Pallas kernels  36.2 us (98%)
  between operations  0.64 us (2%)
    pallas_call x1, Pallas kernels, per_device(): pl.pallas_call(functools.partial(kernel, n), out_shape=(pltpu.VMEM(fine_r...  35.4 us

profile of v3, /device:TPU:0, one launch (start us, length us, event | category | flops | bytes accessed | tf_op | source)
XLA Modules:
  0.0 36.8 jit_solution(17148573224124012542)
XLA Ops:
  0.6 35.4 %shard_map.86 = (bf16[1024,128]{1,0:T(8,128)(2,1)S(1)}, f32[128,128]{1,0:T(8,128)S(1)}) custom-call(s32[48]{0:T(128)} %cols_hbm.1, s32[1,8]{1,0:T(1,128)} %adj_hbm.1, bf16[8,128,128]{2,1,0:T(8,128)(2,1)} %bitcast.3, bf16[1024,128]{1,0:T(8,128)(2,1)} %f_hbm.1, s32[8,512]{1,0:T(8,128)} %bitcast.4, f32[8,128]{1,0:T(8,128)} %bitcast.5, ...), custom_call_target="tpu_custom_call" | custom-call | tf_op jit(solution)/shard_map/pallas_call | solution.py:258
  36.1 0.7 %shard_map.87 = (bf16[1024,128]{1,0:T(8,128)(2,1)}, f32[128,128]{1,0:T(8,128)}) custom-call(bf16[1024,128]{1,0:T(8,128)(2,1)S(1)} %get-tuple-element.4.fine_in, f32[128,128]{1,0:T(8,128)S(1)} %get-tuple-element.5.coarse_in), custom_call_target="tpu_custom_call" | custom-call | tf_op jit(solution)/shard_map/pallas_call | solution.py:306

commit v4 on v3

--- a/solution.py
+++ b/solution.py
@@ -12,11 +12,12 @@
 OFFSETS = (1, 2, 4, 8, -1, -2, -4, -8)
 SEND_ORDER = (1, 5, 2, 6, 0, 4, 3, 7)
 TAKE_ORDER = (4, 0, 5, 1, 6, 2, 7, 3)
-LAST_ORDER = (0, 1, 2, 3, 7, 6, 5, 4)
+LAST_ORDER = (0, 1, 3, 2, 7, 6, 4, 5)
 FLY_ORDER = (0, 1, 2, 3, 4, 5, 6, 7)
 FIRST_ORDER = (0, 1, 2, 3, 4, 5, 6, 7)
 MEET_ORDER = (0, 4, 1, 5, 2, 6, 3, 7)
 EARLY = 1
+FIRST_AFTER = 3
 TAKE_WORK = ((4,), (0,), (5, 11), (1, 8), (), (), (), ())
 MID_WORK = ()
 LATE_WORK = (6, 2, 7, 3, 9, 10)
@@ -132,8 +133,6 @@
     first = coarse_rhs / CHEB_CENTER
     first_high, first_low = halves(first)
     f_send[...] = first_high
-    for slot in FIRST_ORDER:
-        f_copies[slot].start()
 
     for load in loads[3:]:
         load.wait()
@@ -196,6 +195,9 @@
         t_own[slot] = product
         t_send[slot] = product.astype(BF16)
         t_copies[slot].start()
+        if place == FIRST_AFTER:
+            for other in FIRST_ORDER:
+                f_copies[other].start()
         work(TAKE_WORK[place])
     image = own_apply(first_high, first_low)
     weights = [adj_ref[0, slot].astype(F32) for slot in range(slots)]

time: 37 us -> 36.5 us (0.986)
  Pallas kernels: 36.2 us -> 35.6 us
    pallas_call x1, Pallas kernels: 35.4 us -> 34.9 us  [per_device(): pl.pallas_call(functools.partial(kernel, n), out_shape=(pltpu.VMEM(fine_r...]
where the time goes in v4:
time: 36.5 us; the launch traced here: 36.3 us
  Pallas kernels  35.6 us (98%)
  between operations  0.64 us (2%)
    pallas_call x1, Pallas kernels, per_device(): pl.pallas_call(functools.partial(kernel, n), out_shape=(pltpu.VMEM(fine_r...  34.9 us
    pallas_call x1, Pallas kernels, per_device(): pl.pallas_call(deliver, out_shape=(jax.ShapeDtypeStruct(fine.shape, fine....  0.74 us

profile of v4, /device:TPU:0, one launch (start us, length us, event | category | flops | bytes accessed | tf_op | source)
XLA Modules:
  0.0 36.3 jit_solution(14483644223214298688)
XLA Ops:
  0.6 34.9 %shard_map.86 = (bf16[1024,128]{1,0:T(8,128)(2,1)S(1)}, f32[128,128]{1,0:T(8,128)S(1)}) custom-call(s32[48]{0:T(128)} %cols_hbm.1, s32[1,8]{1,0:T(1,128)} %adj_hbm.1, bf16[8,128,128]{2,1,0:T(8,128)(2,1)} %bitcast.3, bf16[1024,128]{1,0:T(8,128)(2,1)} %f_hbm.1, s32[8,512]{1,0:T(8,128)} %bitcast.4, f32[8,128]{1,0:T(8,128)} %bitcast.5, ...), custom_call_target="tpu_custom_call" | custom-call | tf_op jit(solution)/shard_map/pallas_call | solution.py:260
  35.5 0.7 %shard_map.87 = (bf16[1024,128]{1,0:T(8,128)(2,1)}, f32[128,128]{1,0:T(8,128)}) custom-call(bf16[1024,128]{1,0:T(8,128)(2,1)S(1)} %get-tuple-element.4.fine_in, f32[128,128]{1,0:T(8,128)S(1)} %get-tuple-element.5.coarse_in), custom_call_target="tpu_custom_call" | custom-call | tf_op jit(solution)/shard_map/pallas_call | solution.py:308
